TPU v7x, 512 devices: a whole 4x4x16 slice. The times are simulated.
512 devices in a mesh: wide: 64 (over z, x), narrow: 8 (over y, core).
Axes of the slice: x: 4, y: 4, z: 16, core: 2. Of those that a mesh axis runs over, the one named last changes fastest.
Arguments:
- hidden: bfloat16 [2048, 8192], P('wide', 'narrow'), may hold values from -6 to 6
- norm_gain: float32 [8192], P('narrow'), may hold values from 0.1 to 1.9
- head_weight: bfloat16 [8192, 32000], P('narrow', 'wide'), may hold values from -0.24 to 0.24
- diff_rows: bfloat16 [64, 8, 8, 32000], P('wide', 'narrow'), may hold values from -6 to 480
- slot_request: int32 [64, 8, 8], replicated, may hold values from 0 to 2047, as said below
- slot_code: int32 [64, 8, 8], replicated, may hold values from 1 to 8
- slot_count: int32 [64, 8], replicated, may hold values from 1 to 8, as said below
Outputs:
- log_probs: float32 [2048, 32000], P('narrow', 'wide')
Inputs may be any that keep to these rules, and one draw needn't show every extreme that they name: `slot_request`: within one pair, every request is named at most once. `slot_count`: slots at or beyond the count hold no row to use; in every draw some device uses all 8 slots.
All inputs are finite; a program needn't handle non-finite values.
Results may differ from a plain program's by a relative error of at most 0.0003.
Values may be sent and summed in bfloat16 or wider, within the bound.
A program may use at most 64 MiB of HBM per device.

v0:
```python
import jax
import jax.numpy as jnp
from jax import lax
from jax.sharding import PartitionSpec as P

D = 8192
epsilon = 1e-05


def combined_all(part, axis, combine):
    gathered = jax.tree.map(lambda a: lax.all_gather(a, axis), part)

    def take(source):
        return jax.tree.map(lambda a: lax.dynamic_index_in_dim(a, source, 0, False), gathered)

    return lax.fori_loop(
        1, lax.axis_size(axis), lambda source, state: combine(state, take(source)), take(0)
    )


def merge_pair(earlier, later):
    row_peak = jnp.maximum(earlier[0], later[0])
    summed = earlier[1] * jnp.exp(earlier[0] - row_peak) + later[1] * jnp.exp(later[0] - row_peak)
    return (row_peak, summed)


def body(hidden, norm_gain, head_weight, diff_rows, slot_request, slot_code, slot_count):
    values = hidden.astype(jnp.float32)
    squares = lax.psum(jnp.sum(values * values, axis=1), "narrow")
    scales = lax.rsqrt(squares / D + epsilon)
    normed = (values * scales[:, None] * norm_gain[None, :]).astype(jnp.bfloat16)
    partial_value = jnp.dot(
        lax.all_gather(normed, "wide", axis=0, tiled=True),
        head_weight,
        preferred_element_type=jnp.float32,
    )
    row_block = diff_rows[0, 0]
    arrived = lax.all_to_all(row_block, "wide", split_axis=1, concat_axis=0, tiled=True)
    slot_total = row_block.shape[0]
    active = jnp.arange(slot_total, dtype=jnp.int32)[None, None, :] < slot_count[:, :, None]
    weights = jnp.where(active, slot_code, 0).astype(jnp.float32) * 0.25
    base_block = lax.psum_scatter(partial_value, "narrow", scatter_dimension=0, tiled=True)
    owner_slices = lax.all_gather(arrived, "narrow", axis=0, tiled=True)
    targets = jnp.transpose(slot_request, (1, 0, 2)).reshape(-1)
    factor_all = jnp.transpose(weights, (1, 0, 2)).reshape(-1)
    block_rows = base_block.shape[0]
    offsets = targets - lax.axis_index("narrow") * block_rows
    owned = (offsets >= 0) & (offsets < block_rows)
    factors = jnp.where(owned, factor_all, 0.0)
    target_rows = jnp.where(owned, offsets, 0)
    own_block = base_block.at[target_rows].add(owner_slices.astype(jnp.float32) * factors[:, None])
    local_peak = jnp.max(own_block, axis=1)
    local_mass = jnp.sum(jnp.exp(own_block - local_peak[:, None]), axis=1)
    row_peak, row_mass = combined_all((local_peak, local_mass), "wide", merge_pair)
    log_total = row_peak + jnp.log(row_mass)
    return own_block - log_total[:, None]


def solution(mesh):
    placed = (
        P("wide", "narrow"),
        P("narrow"),
        P("narrow", "wide"),
        P("wide", "narrow", None, None),
        P(),
        P(),
        P(),
    )
    return jax.shard_map(
        body, mesh=mesh, in_specs=placed, out_specs=P("narrow", "wide"), check_vma=False
    )
```

profile of v0, /device:TPU:32, one launch (start us, length us, event | category | flops | bytes accessed | tf_op | source)
XLA Modules:
  0.0 463.4 jit_solution(9681761703783635985)
XLA Ops:
  6.5 0.0 copy-start
  6.5 1.0 fusion.4
  7.6 14.9 %psum.7 = f32[32]{0:T(128)S(1)} all-reduce(f32[32]{0:T(128)S(1)} %fusion.4), channel_id=1, replica_groups=mesh['wide'=64,'narrow'=8] {'narrow'}, use_global_device_ids=true, to_apply=%region_1.0 | all-reduce | flops 32 | bytes 256 | tf_op jit(solution)/shard_map/psum | solution.py:29
  22.5 1.6 fusion.6
  24.0 0.0 all-gather.7.cloned.1.call-update
  24.0 0.0 reduce-scatter.2.cloned.1.call-start
  24.1 147.9 %all-gather.7.cloned.1.call-done = bf16[2048,1024]{1,0:T(8,128)(2,1)} async-done(((bf16[32,1024]{1,0:T(8,128)(2,1)}), bf16[2048,1024]{1,0:T(8,128)(2,1)}) %all-gather.7.cloned.1.call-update) | async-done | bytes 4194320 | tf_op jit(solution)/shard_map/all_gather | solution.py:33
  172.0 6.5 %fusion.7 = f32[2048,500]{0,1:T(8,128)} fusion(bf16[2048,1024]{1,0:T(8,128)(2,1)} %all-gather.7.cloned.1.call-done, bf16[1024,500]{0,1:T(8,128)(2,1)S(1)} %copy-done), kind=kOutput, calls=%fused_computation.24 | convolution fusion | flops 2097152000 | bytes 9314304 | tf_op jit(solution)/shard_map/dot_general | solution.py:32
  178.5 0.0 reduce-scatter.2.cloned.1.call-update
  178.5 0.0 all-gather.9.cloned.1.call-start
  178.6 1.0 copy-done.1
  179.5 1.1 all_to_all.14
  180.7 0.3 copy.20
  181.0 32.8 %all_to_all.19 = bf16[8,64,500]{2,0,1:T(8,128)(2,1)} all-to-all(bf16[8,64,500]{2,0,1:T(8,128)(2,1)S(1)} %copy.20), channel_id=1, replica_groups=mesh['wide'=64,'narrow'=8] {'wide'}, dimensions={1} | all-to-all | bytes 1024000 | tf_op jit(solution)/shard_map/all_to_all | solution.py:38
  213.8 0.0 all-gather.9.cloned.1.call-update
  213.8 0.1 copy.19
  214.0 0.2 sub.63
  214.1 0.0 copy-done.3
  214.2 0.0 copy-done.4
  214.2 0.1 copy.21
  214.3 0.2 select_n.54
  214.5 5.4 %reduce-scatter.2.cloned.1.call-done = f32[256,500]{0,1:T(8,128)} async-done(((f32[2048,500]{0,1:T(8,128)}), f32[256,500]{0,1:T(8,128)}) %reduce-scatter.2.cloned.1.call-update) | async-done | bytes 512016 | tf_op jit(solution)/shard_map/reduce_scatter | solution.py:42
  219.9 1.2 copy.22
  221.1 39.4 %all-gather.9.cloned.1.call-done = bf16[4096,500]{1,0:T(8,128)(2,1)} async-done(((bf16[512,500]{1,0:T(8,128)(2,1)}), bf16[4096,500]{1,0:T(8,128)(2,1)}) %all-gather.9.cloned.1.call-update) | async-done | bytes 4096016 | tf_op jit(solution)/shard_map/all_gather | solution.py:43
  260.5 28.5 %scatter_custom_fusion = f32[256,500]{1,0:T(8,128)S(1)} fusion(f32[256,500]{1,0:T(8,128)S(1)} %copy.22, s32[4096]{0:T(1024)S(1)} %bitcast.35, bf16[4096,500]{1,0:T(8,128)(2,1)} %all-gather.9.cloned.1.call-done, f32[4096]{0:T(1024)S(1)} %select_n.54), kind=kCustom, calls=%fused_computation.4 | custom fusion | flops 6144000 | bytes 4624384 | tf_op jit(solution)/shard_map/scatter-add | solution.py:51
  288.9 0.2 copy.23
  289.1 0.1 reduce_max.9
  289.3 0.2 exponential_reduce_fusion
  289.5 82.5 %all-gather.2 = f32[64,1,256]{2,1,0:T(1,128)S(1)} all-gather(f32[1,1,256]{2,1,0:T(1,128)S(1)} %bitcast.36), channel_id=2, replica_groups=mesh['wide'=64,'narrow'=8] {'wide'}, dimensions={0}, use_global_device_ids=true | all-gather | bytes 66560 | tf_op jit(solution)/shard_map/all_gather | solution.py:11
  372.0 80.4 %all-gather.3 = f32[64,1,256]{2,1,0:T(1,128)S(1)} all-gather(f32[1,1,256]{2,1,0:T(1,128)S(1)} %bitcast.37), channel_id=3, replica_groups=mesh['wide'=64,'narrow'=8] {'wide'}, dimensions={0}, use_global_device_ids=true | all-gather | bytes 66560 | tf_op jit(solution)/shard_map/all_gather | solution.py:11
  452.4 3.6 while.17
  456.1 0.8 broadcast_subtract_fusion
  (142 shorter events, 2.1 us)
Async XLA Ops:
  6.5 165.5 %copy-start = (bf16[1024,500]{0,1:T(8,128)(2,1)S(1)}, bf16[1024,500]{0,1:T(8,128)(2,1)}, u32[]{:S(2)}) copy-start(bf16[1024,500]{0,1:T(8,128)(2,1)} %param.11) | copy-start | bytes 3072004
  6.5 165.5 %all-gather.7.cloned.1.call-start = ((), (), s32[]{:S(2)}) async-start(), calls=%async_computation.2 | async-start | bytes 4259840 | tf_op jit(solution)/shard_map/all_gather | solution.py:33
  24.0 195.8 %reduce-scatter.2.cloned.1.call-start = ((), (), s32[]{:S(2)}) async-start(), calls=%async_computation.3 | async-start | bytes 4644864 | tf_op jit(solution)/shard_map/reduce_scatter | solution.py:42
  178.5 1.0 copy-start.1
  178.5 35.3 %copy-start.2 = (s32[64,8,8]{0,2,1:T(8,128)S(1)}, s32[64,8,8]{0,2,1:T(8,128)}, u32[]{:S(2)}) copy-start(s32[64,8,8]{0,2,1:T(8,128)} %param.13) | copy-start | bytes 49156
  178.5 35.7 %copy-start.3 = (s32[64,8,8]{0,2,1:T(8,128)S(1)}, s32[64,8,8]{0,2,1:T(8,128)}, u32[]{:S(2)}) copy-start(s32[64,8,8]{0,2,1:T(8,128)} %param.14) | copy-start | bytes 49156
  178.5 35.7 %copy-start.4 = (s32[64,8]{0,1:T(8,128)S(1)}, s32[64,8]{0,1:T(8,128)}, u32[]{:S(2)}) copy-start(s32[64,8]{0,1:T(8,128)} %param.15) | copy-start | bytes 6148
  178.5 82.0 %all-gather.9.cloned.1.call-start = ((), (), s32[]{:S(2)}) async-start(), calls=%async_computation.4 | async-start | bytes 4718592 | tf_op jit(solution)/shard_map/all_gather | solution.py:43
Sparse Core Ops, SparseCore 0:
  24.2 147.8 all-gather.6
  178.6 41.1 reduce-scatter.1
  222.3 38.1 all-gather.8
where the time goes:
time: 464 us; the launch traced here: 463 us
  blocking collectives  211 us (45%)
  waiting for transfers between devices  193 us (42%)
  other arithmetic  33.6 us (7%)
  between operations  13.3 us (3%)
  matrix products  6.47 us (1%)
  local copies, waits for them, and re-layouts  5.1 us (1%)
    all_gather x2, blocking collectives, combined_all(): gathered = jax.tree.map(lambda a: lax.all_gather(a, axis), part)  163 us
    all_gather x1, waiting for transfers between devices, body(): lax.all_gather(normed, 'wide', axis=0, tiled=True)  148 us
    all_gather x1, waiting for transfers between devices, body(): owner_slices = lax.all_gather(arrived, 'narrow', axis=0, tiled=True)  39.4 us
    all_to_all x1, blocking collectives, body(): lax.all_to_all(row_block, 'wide', split_axis=1, concat_axis=0, tiled=True)  32.8 us
    scatter-add x1, other arithmetic, body(): base_block.at[target_rows]  28.5 us
    psum x1, blocking collectives, body(): squares = lax.psum(jnp.sum(values * values, axis=1), 'narrow')  14.9 us
  transfers between devices with their start and end apart: 3, of which 3 were waited for; matrix products, arithmetic and copies ran while one was open for 0% of the time, Pallas kernels for 0%

commit v1 on v0

--- a/solution.py
+++ b/solution.py
@@ -2,6 +2,7 @@
 import jax.numpy as jnp
 from jax import lax
 from jax.sharding import PartitionSpec as P
+from jax.lax import all_to_all, axis_size
 
 D = 8192
 epsilon = 1e-05
@@ -30,7 +31,15 @@
     scales = lax.rsqrt(squares / D + epsilon)
     normed = (values * scales[:, None] * norm_gain[None, :]).astype(jnp.bfloat16)
     partial_value = jnp.dot(
-        lax.all_gather(normed, "wide", axis=0, tiled=True),
+        jnp.concatenate(
+            all_to_all(
+                jnp.stack([normed] * axis_size("wide"), axis=0),
+                axis_name="wide",
+                split_axis=0,
+                concat_axis=0,
+            ),
+            axis=0,
+        ),
         head_weight,
         preferred_element_type=jnp.float32,
     )

time: 464 us -> 516 us (1.11)
  blocking collectives: 211 us -> 418 us
  waiting for transfers between devices: 193 us -> 39.1 us
    all_to_all x0 -> x1, blocking collectives: none -> 204 us  [body(): all_to_all(jnp.stack([normed] * axis_size('wide'), axis=0), axis_name='wi...]
    all_gather x1 -> x0, waiting for transfers between devices: 148 us -> none  [body(): lax.all_gather(normed, 'wide', axis=0, tiled=True)]
    reduce_scatter x1, waiting for transfers between devices: 5.36 us -> 0.02 us  [body(): lax.psum_scatter(partial_value, 'narrow', scatter_dimension=0, tiled=True)]
  transfers between devices with their start and end apart: 3 -> 2, of which waited for: 3 -> 1; matrix products, arithmetic and copies ran while one was open for 0% -> 0% of each run, Pallas kernels for 0% -> 0%
where the time goes in v1:
time: 516 us; the launch traced here: 515 us
  blocking collectives  418 us (81%)
  waiting for transfers between devices  39.1 us (8%)
  other arithmetic  33 us (6%)
  between operations  13.6 us (3%)
  local copies, waits for them, and re-layouts  5.62 us (1%)
    all_to_all x1, blocking collectives, body(): all_to_all(jnp.stack([normed] * axis_size('wide'), axis=0), axis_name='wi...  204 us
    all_gather x2, blocking collectives, combined_all(): gathered = jax.tree.map(lambda a: lax.all_gather(a, axis), part)  163 us
    all_gather x1, waiting for transfers between devices, body(): owner_slices = lax.all_gather(arrived, 'narrow', axis=0, tiled=True)  39 us
    all_to_all x1, blocking collectives, body(): lax.all_to_all(row_block, 'wide', split_axis=1, concat_axis=0, tiled=True)  36.3 us
    scatter-add x1, other arithmetic, body(): base_block.at[target_rows]  28.5 us
    psum x1, blocking collectives, body(): squares = lax.psum(jnp.sum(values * values, axis=1), 'narrow')  14.9 us
  transfers between devices with their start and end apart: 2, of which 1 were waited for; matrix products, arithmetic and copies ran while one was open for 0% of the time, Pallas kernels for 0%

profile of v1, /device:TPU:32, one launch (start us, length us, event | category | flops | bytes accessed | tf_op | source)
XLA Modules:
  0.0 515.5 jit_solution(10978570041285508463)
XLA Ops:
  6.5 0.0 copy-start
  6.5 0.0 reduce-scatter.2.cloned.1.call-start
  6.5 1.0 fusion.4
  7.6 14.9 %psum.7 = f32[32]{0:T(128)S(1)} all-reduce(f32[32]{0:T(128)S(1)} %fusion.4), channel_id=1, replica_groups=mesh['wide'=64,'narrow'=8] {'narrow'}, use_global_device_ids=true, to_apply=%region_1.0 | all-reduce | flops 32 | bytes 256 | tf_op jit(solution)/shard_map/psum | solution.py:30
  22.5 0.9 fusion.6
  23.4 0.5 stack.2
  23.9 204.2 %all_to_all.24 = bf16[64,32,1024]{2,1,0:T(8,128)(2,1)S(1)} all-to-all(bf16[64,32,1024]{2,1,0:T(8,128)(2,1)S(1)} %stack.2), channel_id=1, replica_groups=mesh['wide'=64,'narrow'=8] {'wide'}, dimensions={0} | all-to-all | bytes 8388608 | tf_op jit(solution)/shard_map/all_to_all | solution.py:35
  228.1 0.0 copy-done
  228.2 4.3 fusion.7
  232.5 0.0 reduce-scatter.2.cloned.1.call-update
  232.5 0.0 all-gather.6.cloned.1.call-start
  232.5 1.0 copy-done.1
  233.5 1.1 all_to_all.18
  234.6 0.3 copy.20
  234.9 36.3 %all_to_all.25 = bf16[8,64,500]{2,0,1:T(8,128)(2,1)} all-to-all(bf16[8,64,500]{2,0,1:T(8,128)(2,1)S(1)} %copy.20), channel_id=1, replica_groups=mesh['wide'=64,'narrow'=8] {'wide'}, dimensions={1} | all-to-all | bytes 1024000 | tf_op jit(solution)/shard_map/all_to_all | solution.py:47
  271.2 0.0 all-gather.6.cloned.1.call-update
  271.2 0.0 copy-done.2
  271.3 0.1 copy.19
  271.4 0.2 sub.63
  271.6 0.1 copy.21
  271.7 0.2 select_n.54
  271.9 0.0 reduce-scatter.2.cloned.1.call-done
  272.0 1.2 copy.22
  273.2 39.0 %all-gather.6.cloned.1.call-done = bf16[4096,500]{1,0:T(8,128)(2,1)} async-done(((bf16[512,500]{1,0:T(8,128)(2,1)}), bf16[4096,500]{1,0:T(8,128)(2,1)}) %all-gather.6.cloned.1.call-update) | async-done | bytes 4096016 | tf_op jit(solution)/shard_map/all_gather | solution.py:52
  312.2 28.5 %scatter_custom_fusion = f32[256,500]{1,0:T(8,128)S(1)} fusion(f32[256,500]{1,0:T(8,128)S(1)} %copy.22, s32[4096]{0:T(1024)S(1)} %bitcast.37, bf16[4096,500]{1,0:T(8,128)(2,1)} %all-gather.6.cloned.1.call-done, f32[4096]{0:T(1024)S(1)} %select_n.54), kind=kCustom, calls=%fused_computation.4 | custom fusion | flops 6144000 | bytes 4624384 | tf_op jit(solution)/shard_map/scatter-add | solution.py:60
  340.7 0.2 copy.23
  340.9 0.1 reduce_max.9
  341.0 0.2 exponential_reduce_fusion
  341.2 82.5 %all-gather.2 = f32[64,1,256]{2,1,0:T(1,128)S(1)} all-gather(f32[1,1,256]{2,1,0:T(1,128)S(1)} %bitcast.38), channel_id=2, replica_groups=mesh['wide'=64,'narrow'=8] {'wide'}, dimensions={0}, use_global_device_ids=true | all-gather | bytes 66560 | tf_op jit(solution)/shard_map/all_gather | solution.py:12
  423.7 80.4 %all-gather.3 = f32[64,1,256]{2,1,0:T(1,128)S(1)} all-gather(f32[1,1,256]{2,1,0:T(1,128)S(1)} %bitcast.39), channel_id=3, replica_groups=mesh['wide'=64,'narrow'=8] {'wide'}, dimensions={0}, use_global_device_ids=true | all-gather | bytes 66560 | tf_op jit(solution)/shard_map/all_gather | solution.py:12
  504.1 3.6 while.17
  507.8 0.8 broadcast_subtract_fusion
  (141 shorter events, 2.1 us)
Async XLA Ops:
  6.5 221.6 %copy-start = (bf16[1024,500]{0,1:T(8,128)(2,1)S(1)}, bf16[1024,500]{0,1:T(8,128)(2,1)}, u32[]{:S(2)}) copy-start(bf16[1024,500]{0,1:T(8,128)(2,1)} %param.11) | copy-start | bytes 3072004
  6.5 265.4 %reduce-scatter.2.cloned.1.call-start = ((), (), s32[]{:S(2)}) async-start(), calls=%async_computation.3 | async-start | bytes 4644864 | tf_op jit(solution)/shard_map/reduce_scatter | solution.py:51
  232.5 1.0 copy-start.1
  232.5 38.8 %copy-start.2 = (s32[64,8,8]{0,2,1:T(8,128)S(1)}, s32[64,8,8]{0,2,1:T(8,128)}, u32[]{:S(2)}) copy-start(s32[64,8,8]{0,2,1:T(8,128)} %param.13) | copy-start | bytes 49156
  232.5 39.1 %copy-start.3 = (s32[64,8,8]{0,2,1:T(8,128)S(1)}, s32[64,8,8]{0,2,1:T(8,128)}, u32[]{:S(2)}) copy-start(s32[64,8,8]{0,2,1:T(8,128)} %param.14) | copy-start | bytes 49156
  232.5 39.1 %copy-start.4 = (s32[64,8]{0,1:T(8,128)S(1)}, s32[64,8]{0,1:T(8,128)}, u32[]{:S(2)}) copy-start(s32[64,8]{0,1:T(8,128)} %param.15) | copy-start | bytes 6148
  232.5 79.7 %all-gather.6.cloned.1.call-start = ((), (), s32[]{:S(2)}) async-start(), calls=%async_computation.4 | async-start | bytes 4718592 | tf_op jit(solution)/shard_map/all_gather | solution.py:52
Sparse Core Ops, SparseCore 0:
  232.6 38.5 reduce-scatter.1
  273.6 38.5 all-gather.5
